TPU v7x, 32 devices: a whole 2x2x4 slice. The times are simulated.
32 devices in a mesh: gx: 2 (over x), yz: 16 (over z, y, core).
Axes of the slice: x: 2, y: 2, z: 4, core: 2. Of those that a mesh axis runs over, the one named last changes fastest.
Arguments:
- tensor: float32 [4, 512, 32, 32], P(None, 'gx', 'yz'), may hold values from -40 to 40
- start_basis: float32 [96, 512], replicated, may hold values from -6 to 6
Outputs:
- core_tensor: float32 [32, 32, 384], P(('gx', 'yz'))
- factor: float32 [96, 512], replicated
All inputs are finite; a program needn't handle non-finite values.
Results may differ from a plain program's by a relative error of at most 0.00012.
Values sent between devices are 32-bit elements; how exact they have to be, the bound alone decides.
A program may use at most 64 MiB of HBM per device.

v0:
```python
import jax
import jax.numpy as jnp
from jax import lax
from jax.sharding import PartitionSpec as P


def orthonormal(image_rows):
    small_gram = jnp.dot(image_rows, image_rows.T, precision=lax.Precision.HIGHEST)
    lower_factor = jnp.linalg.cholesky(small_gram)
    return lax.linalg.triangular_solve(lower_factor, image_rows, left_side=True, lower=True)


def fibre_gram(left_part, right_part):
    return lax.dot_general(
        left_part, right_part, (((0, 2, 3), (0, 2, 3)), ((), ())), precision=lax.Precision.HIGHEST
    )


def local(tensor, start_basis):
    regrouped = lax.all_to_all(tensor, "gx", split_axis=2, concat_axis=1, tiled=True)
    species, width_x, lines, cells_z = regrouped.shape
    cell_count = species * lines * lax.axis_size("gx") * lax.axis_size("yz") * cells_z
    gram_matrix = lax.psum(fibre_gram(regrouped, regrouped), ("gx", "yz")) / cell_count
    basis = start_basis
    for repeat in range(2):
        basis = orthonormal(jnp.dot(basis, gram_matrix, precision=lax.Precision.HIGHEST))
    core_local = jnp.einsum("kx,sxyz->zysk", basis, regrouped, precision=lax.Precision.HIGHEST)
    core_local = core_local.reshape(cells_z, lines, species * basis.shape[0])
    core_tensor = lax.all_to_all(
        lax.all_to_all(core_local, "gx", split_axis=0, concat_axis=1, tiled=True),
        "yz",
        split_axis=0,
        concat_axis=1,
        tiled=True,
    )
    return (core_tensor, basis)


def solution(mesh):
    placed = (P(None, "gx", "yz", None), P())
    return jax.shard_map(
        local,
        mesh=mesh,
        in_specs=placed,
        out_specs=(P(("gx", "yz"), None, None), P()),
        check_vma=False,
    )
```

profile of v0, /device:TPU:0, one launch (start us, length us, event | category | flops | bytes accessed | tf_op | source)
XLA Modules:
  0.0 216.7 jit_solution(6574498621706970048)
XLA Ops:
  7.2 0.0 copy-start
  7.2 0.0 all-reduce.2.cloned.1.call-start
  7.2 1.0 copy.16
  8.2 9.2 %all_to_all.45 = f32[4,256,2,32]{1,3,0,2:T(8,128)S(1)} all-to-all(f32[4,256,2,32]{1,3,0,2:T(8,128)S(1)} %copy.16), channel_id=1, replica_groups=mesh['gx'=2,'yz'=16] {'gx'}, dimensions={2} | all-to-all | bytes 524288 | tf_op jit(solution)/shard_map/all_to_all | solution.py:20
  17.4 0.2 copy.17
  17.7 0.2 reshape.30
  17.9 2.1 convolution_bitcast_fusion
  19.9 0.0 all-reduce.2.cloned.1.call-update
  20.0 131.3 %all-reduce.2.cloned.1.call-done = f32[512,512]{1,0:T(8,128)} async-done(((f32[512,512]{1,0:T(8,128)}), f32[512,512]{1,0:T(8,128)}) %all-reduce.2.cloned.1.call-update) | async-done | bytes 1048592 | tf_op jit(solution)/shard_map/psum | solution.py:23
  151.3 2.1 fusion.2
  153.4 0.3 fusion.19
  153.7 0.1 copy.18
  153.8 8.8 %cholesky.44 = f32[96,96]{1,0:T(8,128)S(1)} custom-call(f32[96,96]{1,0:T(8,128)S(1)} %fusion.14), custom_call_target="Cholesky" | custom-call | tf_op jit(solution)/shard_map/jit(cholesky)/cholesky | solution.py:9
  162.6 0.6 compare_reduce_fusion.1
  163.3 0.7 fusion.8
  163.9 7.4 %custom-call.6 = f32[1,96,96]{1,2,0:T(8,128)S(1)} custom-call(f32[1,96,96]{2,1,0:T(8,128)S(1)} %fusion.8), custom_call_target="InvertDiagBlocksLowerTriangular" | custom-call | tf_op jit(solution)/shard_map/triangular_solve/custom-call.0 | solution.py:10
  171.3 0.4 fusion.6
  171.7 0.8 fusion
  172.5 0.3 fusion.20
  172.8 0.1 copy.19
  172.9 8.8 %cholesky.55 = f32[96,96]{1,0:T(8,128)S(1)} custom-call(f32[96,96]{1,0:T(8,128)S(1)} %fusion.12), custom_call_target="Cholesky" | custom-call | tf_op jit(solution)/shard_map/jit(cholesky)/cholesky | solution.py:9
  181.7 0.6 compare_reduce_fusion
  182.3 0.7 fusion.9
  183.0 7.4 %custom-call.7 = f32[1,96,96]{1,2,0:T(8,128)S(1)} custom-call(f32[1,96,96]{2,1,0:T(8,128)S(1)} %fusion.9), custom_call_target="InvertDiagBlocksLowerTriangular" | custom-call | tf_op jit(solution)/shard_map/triangular_solve/custom-call.0 | solution.py:10
  190.4 0.4 fusion.10
  190.8 0.0 copy-start.2
  190.8 0.4 fusion.21
  191.1 0.3 copy-done.2
  191.5 0.1 reshape.41
  191.6 6.6 %all_to_all.46 = f32[32,1,384]{2,1,0:T(1,128)S(1)} all-to-all(f32[32,1,384]{2,1,0:T(1,128)S(1)} %reshape.41), channel_id=1, replica_groups=mesh['gx'=2,'yz'=16] {'gx'}, dimensions={0} | all-to-all | bytes 98304 | tf_op jit(solution)/shard_map/all_to_all | solution.py:30
  198.2 10.9 %all_to_all.47 = f32[16,2,384]{2,1,0:T(2,128)S(1)} all-to-all(f32[16,2,384]{2,1,0:T(2,128)S(1)} %copy.22), channel_id=1, replica_groups=mesh['gx'=2,'yz'=16] {'yz'}, dimensions={0} | all-to-all | bytes 98304 | tf_op jit(solution)/shard_map/all_to_all | solution.py:29
  209.2 0.7 all_to_all.41
  (10 shorter events, 0.2 us)
Async XLA Ops:
  7.2 144.1 %copy-start = (f32[96,512]{1,0:T(8,128)S(1)}, f32[96,512]{1,0:T(8,128)}, u32[]{:S(2)}) copy-start(f32[96,512]{1,0:T(8,128)} %param.6) | copy-start | bytes 589828
  7.2 144.1 %all-reduce.2.cloned.1.call-start = ((), (), s32[]{:S(2)}) async-start(), calls=%async_computation.3 | async-start | bytes 2097152 | tf_op jit(solution)/shard_map/psum | solution.py:23
  151.3 20.4 %copy-start.1 = (f32[512,512]{1,0:T(8,128)S(1)}, f32[512,512]{1,0:T(8,128)}, u32[]{:S(2)}) copy-start(f32[512,512]{1,0:T(8,128)} %all-reduce.2.cloned.1.call-done) | copy-start | bytes 3145732
  190.8 0.7 copy-start.2
Sparse Core Ops, SparseCore 0:
  20.1 131.1 all-reduce.1
where the time goes:
time: 217 us
  waiting for transfers between devices  131 us (60%)
  other arithmetic  34.9 us (16%)
  blocking collectives  26.7 us (12%)
  between operations  14.2 us (7%)
  matrix products  6.67 us (3%)
  local copies, waits for them, and re-layouts  2.77 us (1%)
    psum x1, waiting for transfers between devices, local(): lax.psum(fibre_gram(regrouped, regrouped), ('gx', 'yz')) / cell_count  131 us
    another operation x6, other arithmetic, orthonormal(): lower_factor = jnp.linalg.cholesky(small_gram)  18.9 us
    another operation x4, other arithmetic, orthonormal(): lax.linalg.triangular_solve(lower_factor, image_rows, left_side=True, low...  16 us
    all_to_all x1, blocking collectives, local(): lax.all_to_all(lax.all_to_all(core_local, 'gx', split_axis=0, concat_axis...  10.9 us
    all_to_all x1, blocking collectives, local(): lax.all_to_all(tensor, 'gx', split_axis=2, concat_axis=1, tiled=True)  9.21 us
    all_to_all x1, blocking collectives, local(): lax.all_to_all(core_local, 'gx', split_axis=0, concat_axis=1, tiled=True)  6.57 us
  transfers between devices with their start and end apart: 1, of which 1 were waited for; matrix products, arithmetic and copies ran while one was open for 0% of the time, Pallas kernels for 0%

commit v1 on v0

--- a/solution.py
+++ b/solution.py
@@ -20,7 +20,9 @@
     regrouped = lax.all_to_all(tensor, "gx", split_axis=2, concat_axis=1, tiled=True)
     species, width_x, lines, cells_z = regrouped.shape
     cell_count = species * lines * lax.axis_size("gx") * lax.axis_size("yz") * cells_z
-    gram_matrix = lax.psum(fibre_gram(regrouped, regrouped), ("gx", "yz")) / cell_count
+    gram_matrix = (
+        jnp.sum(lax.all_gather(fibre_gram(regrouped, regrouped), ("gx", "yz")), axis=0) / cell_count
+    )
     basis = start_basis
     for repeat in range(2):
         basis = orthonormal(jnp.dot(basis, gram_matrix, precision=lax.Precision.HIGHEST))

time: 217 us -> 290 us (1.34)
  waiting for transfers between devices: 131 us -> 195 us
  other arithmetic: 34.9 us -> 47.2 us
    all_gather x0 -> x1, waiting for transfers between devices: none -> 195 us  [local(): lax.all_gather(fibre_gram(regrouped, regrouped), ('gx', 'yz'))]
    psum x1 -> x0, waiting for transfers between devices: 131 us -> none  [local(): lax.psum(fibre_gram(regrouped, regrouped), ('gx', 'yz')) / cell_count]
    reduce_sum x0 -> x1, other arithmetic: none -> 12.3 us  [local(): jnp.sum(lax.all_gather(fibre_gram(regrouped, regrouped), ('gx', 'yz')), a...]
where the time goes in v1:
time: 290 us
  waiting for transfers between devices  195 us (67%)
  other arithmetic  47.2 us (16%)
  blocking collectives  26 us (9%)
  between operations  14.2 us (5%)
  matrix products  5.31 us (2%)
    all_gather x1, waiting for transfers between devices, local(): lax.all_gather(fibre_gram(regrouped, regrouped), ('gx', 'yz'))  195 us
    another operation x6, other arithmetic, orthonormal(): lower_factor = jnp.linalg.cholesky(small_gram)  18.9 us
    another operation x4, other arithmetic, orthonormal(): lax.linalg.triangular_solve(lower_factor, image_rows, left_side=True, low...  16 us
    reduce_sum x1, other arithmetic, local(): jnp.sum(lax.all_gather(fibre_gram(regrouped, regrouped), ('gx', 'yz')), a...  12.3 us
    all_to_all x1, blocking collectives, local(): lax.all_to_all(lax.all_to_all(core_local, 'gx', split_axis=0, concat_axis...  10.2 us
    all_to_all x1, blocking collectives, local(): lax.all_to_all(tensor, 'gx', split_axis=2, concat_axis=1, tiled=True)  9.21 us
    all_to_all x1, blocking collectives, local(): lax.all_to_all(core_local, 'gx', split_axis=0, concat_axis=1, tiled=True)  6.53 us
  transfers between devices with their start and end apart: 1, of which 1 were waited for; matrix products, arithmetic and copies ran while one was open for 0% of the time, Pallas kernels for 0%

profile of v1, /device:TPU:0, one launch (start us, length us, event | category | flops | bytes accessed | tf_op | source)
XLA Modules:
  0.0 289.9 jit_solution(16687230580008992419)
XLA Ops:
  7.2 0.0 copy-start
  7.2 0.0 all-gather.3.cloned.1.call-start
  7.2 1.0 copy.16
  8.2 9.2 %all_to_all.45 = f32[4,256,2,32]{1,3,0,2:T(8,128)S(1)} all-to-all(f32[4,256,2,32]{1,3,0,2:T(8,128)S(1)} %copy.16), channel_id=1, replica_groups=mesh['gx'=2,'yz'=16] {'gx'}, dimensions={2} | all-to-all | bytes 524288 | tf_op jit(solution)/shard_map/all_to_all | solution.py:20
  17.4 0.2 copy.17
  17.7 0.2 reshape.30
  17.9 2.0 convolution_bitcast_fusion
  19.9 0.0 all-gather.3.cloned.1.call-update
  19.9 194.7 %all-gather.3.cloned.1.call-done = f32[16384,512]{1,0:T(8,128)} async-done(((f32[512,512]{1,0:T(8,128)}), f32[16384,512]{1,0:T(8,128)}) %all-gather.3.cloned.1.call-update) | async-done | bytes 33554448 | tf_op jit(solution)/shard_map/all_gather | solution.py:24
  214.7 12.3 %reduce_sum.9 = f32[512,512]{1,0:T(8,128)S(1)} reduce(f32[32,512,512]{2,1,0:T(8,128)} %bitcast.57, f32[]{:T(128)} %constant.32.clone.1), dimensions={0}, to_apply=%region_0.0 | reduce | flops 8126464 | bytes 34603012 | tf_op jit(solution)/shard_map/reduce_sum | solution.py:24
  226.9 0.8 fusion.2
  227.7 0.3 fusion.19
  228.0 0.1 copy.18
  228.2 8.8 %cholesky.44 = f32[96,96]{1,0:T(8,128)S(1)} custom-call(f32[96,96]{1,0:T(8,128)S(1)} %fusion.14), custom_call_target="Cholesky" | custom-call | tf_op jit(solution)/shard_map/jit(cholesky)/cholesky | solution.py:9
  237.0 0.6 compare_reduce_fusion.1
  237.6 0.7 fusion.8
  238.3 7.4 %custom-call.6 = f32[1,96,96]{1,2,0:T(8,128)S(1)} custom-call(f32[1,96,96]{2,1,0:T(8,128)S(1)} %fusion.8), custom_call_target="InvertDiagBlocksLowerTriangular" | custom-call | tf_op jit(solution)/shard_map/triangular_solve/custom-call.0 | solution.py:10
  245.6 0.4 fusion.6
  246.0 0.8 fusion
  246.8 0.3 fusion.20
  247.1 0.1 copy.19
  247.2 8.8 %cholesky.55 = f32[96,96]{1,0:T(8,128)S(1)} custom-call(f32[96,96]{1,0:T(8,128)S(1)} %fusion.12), custom_call_target="Cholesky" | custom-call | tf_op jit(solution)/shard_map/jit(cholesky)/cholesky | solution.py:9
  256.0 0.6 compare_reduce_fusion
  256.7 0.7 fusion.9
  257.3 7.4 %custom-call.7 = f32[1,96,96]{1,2,0:T(8,128)S(1)} custom-call(f32[1,96,96]{2,1,0:T(8,128)S(1)} %fusion.9), custom_call_target="InvertDiagBlocksLowerTriangular" | custom-call | tf_op jit(solution)/shard_map/triangular_solve/custom-call.0 | solution.py:10
  264.7 0.4 fusion.10
  265.1 0.0 copy-start.1
  265.1 0.4 fusion.21
  265.5 0.1 reshape.42
  265.7 6.5 %all_to_all.46 = f32[32,1,384]{2,1,0:T(1,128)S(1)} all-to-all(f32[32,1,384]{2,1,0:T(1,128)S(1)} %reshape.42), channel_id=1, replica_groups=mesh['gx'=2,'yz'=16] {'gx'}, dimensions={0} | all-to-all | bytes 98304 | tf_op jit(solution)/shard_map/all_to_all | solution.py:32
  272.2 10.2 %all_to_all.47 = f32[16,2,384]{2,1,0:T(2,128)S(1)} all-to-all(f32[16,2,384]{2,1,0:T(2,128)S(1)} %copy.22), channel_id=1, replica_groups=mesh['gx'=2,'yz'=16] {'yz'}, dimensions={0} | all-to-all | bytes 98304 | tf_op jit(solution)/shard_map/all_to_all | solution.py:31
  282.4 0.7 all_to_all.41
  (9 shorter events, 0.2 us)
Async XLA Ops:
  7.2 219.8 %copy-start = (f32[96,512]{1,0:T(8,128)S(1)}, f32[96,512]{1,0:T(8,128)}, u32[]{:S(2)}) copy-start(f32[96,512]{1,0:T(8,128)} %param.6) | copy-start | bytes 589828
  7.2 207.5 %all-gather.3.cloned.1.call-start = ((), (), s32[]{:S(2)}) async-start(), calls=%async_computation.3 | async-start | bytes 34603008 | tf_op jit(solution)/shard_map/all_gather | solution.py:24
  265.1 18.0 %copy-start.1 = (f32[96,512]{1,0:T(8,128)}, f32[96,512]{1,0:T(8,128)S(1)}, u32[]{:S(2)}) copy-start(f32[96,512]{1,0:T(8,128)S(1)} %fusion.10) | copy-start | bytes 589828
Sparse Core Ops, SparseCore 0:
  20.0 194.5 all-gather.2
